TPU v7x, 32 devices: a whole 2x2x4 slice. The times are simulated.
32 devices in a mesh: tm: 8 (over z, x), chan: 4 (over y, core).
Axes of the slice: x: 2, y: 2, z: 4, core: 2. Of those that a mesh axis runs over, the one named last changes fastest.
Arguments:
- samples: bfloat16 [4096, 16384], P('tm', 'chan'), may hold values from -180 to 180
- sketch: bfloat16 [16384, 512], P('chan'), may hold values from -0.046875 to 0.046875
Outputs:
- coords: float32 [4096, 512], P('tm')
- weights: float32 [4096], P('tm')
All inputs are finite; a program needn't handle non-finite values.
Results may differ from a plain program's by a relative error of at most 0.0033.
Values may be sent and summed in bfloat16 or wider, within the bound.
A program may use at most 64 MiB of HBM per device.

v0:
```python
import jax
import jax.numpy as jnp
from jax import lax
from jax.sharding import PartitionSpec as P

C = 16384
ROUNDS = 2


def shards(samples, sketch):
    sketched = lax.psum(jnp.dot(samples, sketch, preferred_element_type=jnp.float32), "chan")
    weights = jnp.ones((samples.shape[0],), jnp.float32)
    coords = jnp.zeros(sketched.shape, jnp.float32)
    for step in range(ROUNDS):
        weighted = ((weights * weights)[:, None] * sketched).astype(jnp.bfloat16)
        local_factor = jnp.einsum(
            "sc,sk->ck", samples, weighted, preferred_element_type=jnp.float32
        )
        factor = lax.psum(local_factor, "tm")
        local_gram = jnp.dot(
            factor.T, factor, precision=lax.Precision.HIGHEST, preferred_element_type=jnp.float32
        )
        gram = lax.psum(local_gram, "chan")
        lower = jnp.linalg.cholesky(gram)
        basis = lax.linalg.triangular_solve(
            lower, factor, left_side=False, lower=True, transpose_a=True
        ).astype(jnp.bfloat16)
        local_coords = jnp.dot(samples, basis, preferred_element_type=jnp.float32)
        coords = lax.psum(local_coords, "chan")
        back = jnp.einsum(
            "sk,ck->sc", coords.astype(jnp.bfloat16), basis, preferred_element_type=jnp.float32
        )
        resid = samples.astype(jnp.float32) - back
        energy = lax.psum(jnp.sum(resid * resid, axis=1), "chan")
        weights = jnp.minimum(1.0, 3.0 / jnp.sqrt(energy / C + 1e-06))
    return (coords, weights)


def solution(mesh):
    in_specs = (P("tm", "chan"), P("chan", None))
    out_specs = (P("tm", None), P("tm"))
    return jax.shard_map(shards, mesh=mesh, in_specs=in_specs, out_specs=out_specs, check_vma=False)
```

profile of v0, /device:TPU:0, one launch (start us, length us, event | category | flops | bytes accessed | tf_op | source)
XLA Modules:
  0.0 1137.1 jit_solution(4831139212829809344)
XLA Ops:
  7.2 6.8 fusion.86
  14.0 38.9 %all-reduce.9.cloned.1.call-done = f32[512,512]{1,0:T(8,128)} async-done(((f32[512,512]{1,0:T(8,128)}), f32[512,512]{1,0:T(8,128)}) %all-reduce.9.cloned.1.call-update) | async-done | bytes 1048592 | tf_op jit(solution)/shard_map/psum | solution.py:11
  53.0 8.1 convolution_bitcast_fusion.1
  61.2 270.9 %all-reduce.11.cloned.1.call-done = f32[4096,512]{0,1:T(8,128)} async-done(((f32[4096,512]{0,1:T(8,128)}), f32[4096,512]{0,1:T(8,128)}) %all-reduce.11.cloned.1.call-update) | async-done | bytes 8388624 | tf_op jit(solution)/shard_map/psum | solution.py:19
  332.0 17.2 %fusion.87 = f32[512,512]{0,1:T(8,128)} fusion(f32[4096,512]{0,1:T(8,128)} %all-reduce.11.cloned.1.call-done), kind=kOutput, calls=%fused_computation.154 | convolution fusion | flops 12884901888 | bytes 9437184 | tf_op jit(solution)/shard_map/dot_general | solution.py:20
  349.5 35.0 %all-reduce.13.cloned.1.call-done = f32[512,512]{0,1:T(8,128)} async-done(((f32[512,512]{0,1:T(8,128)}), f32[512,512]{0,1:T(8,128)}) %all-reduce.13.cloned.1.call-update) | async-done | bytes 1048592 | tf_op jit(solution)/shard_map/psum | solution.py:23
  387.6 11.7 %cholesky.286 = f32[128,128]{1,0:T(8,128)S(1)} custom-call(f32[128,128]{1,0:T(8,128)S(1)} %cholesky.426), custom_call_target="Cholesky" | custom-call | tf_op jit(solution)/shard_map/jit(cholesky)/cholesky | solution.py:24
  399.3 9.8 custom-call.27
  410.0 11.7 %cholesky.305 = f32[128,128]{1,0:T(8,128)S(1)} custom-call(f32[128,128]{1,0:T(8,128)S(1)} %cholesky.430), custom_call_target="Cholesky" | custom-call | tf_op jit(solution)/shard_map/jit(cholesky)/cholesky | solution.py:24
  421.7 10.2 custom-call.28
  432.6 11.7 %cholesky.326 = f32[128,128]{1,0:T(8,128)S(1)} custom-call(f32[128,128]{1,0:T(8,128)S(1)} %cholesky.435), custom_call_target="Cholesky" | custom-call | tf_op jit(solution)/shard_map/jit(cholesky)/cholesky | solution.py:24
  444.9 9.8 custom-call.29
  455.4 11.7 %cholesky.343 = f32[128,128]{1,0:T(8,128)S(1)} custom-call(f32[128,128]{1,0:T(8,128)S(1)} %convolution_subtract_fusion.9), custom_call_target="Cholesky" | custom-call | tf_op jit(solution)/shard_map/jit(cholesky)/cholesky | solution.py:24
  471.2 7.7 while.4
  478.9 39.3 %custom-call.30 = f32[4,128,128]{1,2,0:T(8,128)S(1)} custom-call(f32[4,128,128]{2,1,0:T(8,128)S(1)} %get-tuple-element.18), custom_call_target="InvertDiagBlocksLowerTriangular" | custom-call | tf_op jit(solution)/shard_map/triangular_solve/custom-call.3 | solution.py:25
  534.3 7.2 fusion.19
  546.8 25.7 %all-reduce.20 = bf16[512,512]{0,1:T(8,128)(2,1)} all-reduce(f32[512,512]{0,1:T(8,128)S(1)} %convolution_bitcast_fusion.3), channel_id=1, replica_groups=mesh['tm'=8,'chan'=4] {'chan'}, use_global_device_ids=true, to_apply=%region_11.14 | all-reduce | flops 262144 | bytes 1572864 | tf_op jit(solution)/shard_map/psum | solution.py:29
  584.7 7.9 convolution_bitcast_fusion
  592.7 270.9 %all-reduce.15.cloned.1.call-done = f32[4096,512]{0,1:T(8,128)} async-done(((f32[4096,512]{0,1:T(8,128)}), f32[4096,512]{0,1:T(8,128)}) %all-reduce.15.cloned.1.call-update) | async-done | bytes 8388624 | tf_op jit(solution)/shard_map/psum | solution.py:19
  863.6 17.2 %fusion.88 = f32[512,512]{0,1:T(8,128)} fusion(f32[4096,512]{0,1:T(8,128)} %all-reduce.15.cloned.1.call-done), kind=kOutput, calls=%fused_computation.155 | convolution fusion | flops 12884901888 | bytes 9437184 | tf_op jit(solution)/shard_map/dot_general | solution.py:20
  881.1 35.1 %all-reduce.17.cloned.1.call-done = f32[512,512]{0,1:T(8,128)} async-done(((f32[512,512]{0,1:T(8,128)}), f32[512,512]{0,1:T(8,128)}) %all-reduce.17.cloned.1.call-update) | async-done | bytes 1048592 | tf_op jit(solution)/shard_map/psum | solution.py:23
  919.2 11.7 %cholesky.358 = f32[128,128]{1,0:T(8,128)S(1)} custom-call(f32[128,128]{1,0:T(8,128)S(1)} %cholesky.439), custom_call_target="Cholesky" | custom-call | tf_op jit(solution)/shard_map/jit(cholesky)/cholesky | solution.py:24
  931.1 9.8 custom-call.31
  941.5 11.7 %cholesky.377 = f32[128,128]{1,0:T(8,128)S(1)} custom-call(f32[128,128]{1,0:T(8,128)S(1)} %cholesky.443), custom_call_target="Cholesky" | custom-call | tf_op jit(solution)/shard_map/jit(cholesky)/cholesky | solution.py:24
  954.5 10.2 custom-call.32
  965.4 11.7 %cholesky.398 = f32[128,128]{1,0:T(8,128)S(1)} custom-call(f32[128,128]{1,0:T(8,128)S(1)} %cholesky.448), custom_call_target="Cholesky" | custom-call | tf_op jit(solution)/shard_map/jit(cholesky)/cholesky | solution.py:24
  977.8 9.8 custom-call.33
  988.2 11.7 %cholesky.415 = f32[128,128]{1,0:T(8,128)S(1)} custom-call(f32[128,128]{1,0:T(8,128)S(1)} %convolution_subtract_fusion.8), custom_call_target="Cholesky" | custom-call | tf_op jit(solution)/shard_map/jit(cholesky)/cholesky | solution.py:24
  1003.4 7.7 while.5
  1011.1 39.3 %custom-call.34 = f32[4,128,128]{1,2,0:T(8,128)S(1)} custom-call(f32[4,128,128]{2,1,0:T(8,128)S(1)} %get-tuple-element.19), custom_call_target="InvertDiagBlocksLowerTriangular" | custom-call | tf_op jit(solution)/shard_map/triangular_solve/custom-call.3 | solution.py:25
  1066.5 7.0 fusion.16
  1078.9 36.6 %all-reduce.19.cloned.1.call-done = f32[512,512]{0,1:T(8,128)} async-done(((f32[512,512]{0,1:T(8,128)}), f32[512,512]{0,1:T(8,128)}) %all-reduce.19.cloned.1.call-update) | async-done | bytes 1048592 | tf_op jit(solution)/shard_map/psum | solution.py:29
  (118 shorter events, 100.9 us)
Async XLA Ops:
  7.2 45.8 %all-reduce.9.cloned.1.call-start = ((), (), s32[]{:S(2)}) async-start(), calls=%async_computation | async-start | bytes 2097152 | tf_op jit(solution)/shard_map/psum | solution.py:11
  14.0 318.0 %all-reduce.11.cloned.1.call-start = ((), (), s32[]{:S(2)}) async-start(), calls=%async_computation.1 | async-start | bytes 16777216 | tf_op jit(solution)/shard_map/psum | solution.py:19
  61.1 323.5 %all-reduce.13.cloned.1.call-start = ((), (), s32[]{:S(2)}) async-start(), calls=%async_computation.2 | async-start | bytes 2097152 | tf_op jit(solution)/shard_map/psum | solution.py:23
  349.3 514.3 %all-reduce.15.cloned.1.call-start = ((), (), s32[]{:S(2)}) async-start(), calls=%async_computation.3 | async-start | bytes 16777216 | tf_op jit(solution)/shard_map/psum | solution.py:19
  527.4 16.1 %copy-start.1 = (f32[4096,128]{0,1:T(8,128)}, f32[4096,128]{0,1:T(8,128)S(1)}, u32[]{:S(2)}) copy-start(f32[4096,128]{0,1:T(8,128)S(1)} %fusion.62) | copy-start | bytes 6291460
  534.3 9.2 copy-start.5
  534.3 10.2 copy-start.2
  543.5 1.0 copy-start.7
  572.5 12.2 %copy-start.6 = (f32[512,512]{1,0:T(8,128)S(1)}, f32[512,512]{1,0:T(8,128)}, u32[]{:S(2)}) copy-start(f32[512,512]{1,0:T(8,128)} %all-reduce.9.cloned.1.call-done) | copy-start | bytes 3145732
  592.6 323.5 %all-reduce.17.cloned.1.call-start = ((), (), s32[]{:S(2)}) async-start(), calls=%async_computation.4 | async-start | bytes 2097152 | tf_op jit(solution)/shard_map/psum | solution.py:23
  880.9 234.7 %all-reduce.19.cloned.1.call-start = ((), (), s32[]{:S(2)}) async-start(), calls=%async_computation.5 | async-start | bytes 2097152 | tf_op jit(solution)/shard_map/psum | solution.py:29
  1059.5 15.9 %copy-start = (f32[4096,128]{0,1:T(8,128)}, f32[4096,128]{0,1:T(8,128)S(1)}, u32[]{:S(2)}) copy-start(f32[4096,128]{0,1:T(8,128)S(1)} %fusion.56) | copy-start | bytes 6291460
  1066.5 9.0 copy-start.4
  1066.5 9.0 copy-start.3
Sparse Core Ops, SparseCore 0:
  14.1 38.8 all-reduce.8
  61.2 270.7 all-reduce.10
  349.4 35.1 all-reduce.12
  592.8 270.8 all-reduce.14
  881.0 35.1 all-reduce.16
  1079.0 36.4 all-reduce.18
where the time goes:
time: 1140 us
  waiting for transfers between devices  688 us (60%)
  other arithmetic  241 us (21%)
  matrix products  128 us (11%)
  blocking collectives  38.2 us (3%)
  local copies, waits for them, and re-layouts  22.2 us (2%)
  between operations  19.7 us (2%)
    psum x2, waiting for transfers between devices, shards(): factor = lax.psum(local_factor, 'tm')  542 us
    another operation x29, other arithmetic, shards(): lower = jnp.linalg.cholesky(gram)  158 us
    another operation x5, other arithmetic, shards(): lax.linalg.triangular_solve(lower, factor, left_side=False, lower=True, t...  79.2 us
    psum x2, waiting for transfers between devices, shards(): gram = lax.psum(local_gram, 'chan')  70.1 us
    another operation x14, matrix products, shards(): lax.linalg.triangular_solve(lower, factor, left_side=False, lower=True, t...  50.1 us
    psum x1, waiting for transfers between devices, shards(): lax.psum(jnp.dot(samples, sketch, preferred_element_type=jnp.float32), 'c...  38.9 us
    psum x1, waiting for transfers between devices, shards(): coords = lax.psum(local_coords, 'chan')  36.6 us
    dot_general x2, matrix products, shards(): jnp.dot(factor.T, factor, precision=lax.Precision.HIGHEST, preferred_elem...  34.5 us
  transfers between devices with their start and end apart: 6, of which 6 were waited for; matrix products, arithmetic and copies ran while one was open for 0% of the time, Pallas kernels for 0%

commit v1 on v0

--- a/solution.py
+++ b/solution.py
@@ -16,7 +16,9 @@
         local_factor = jnp.einsum(
             "sc,sk->ck", samples, weighted, preferred_element_type=jnp.float32
         )
-        factor = lax.psum(local_factor, "tm")
+        factor = local_factor
+        for hop in (1, 2, 4):
+            factor = factor + lax.ppermute(factor, "tm", [(dev, dev ^ hop) for dev in range(8)])
         local_gram = jnp.dot(
             factor.T, factor, precision=lax.Precision.HIGHEST, preferred_element_type=jnp.float32
         )

time: 1140 us -> 2110 us (1.85)
  waiting for transfers between devices: 688 us -> 1590 us
  other arithmetic: 241 us -> 308 us
    ppermute x0 -> x6, waiting for transfers between devices: none -> 1440 us  [shards(): lax.ppermute(factor, 'tm', [(dev, dev ^ hop) for dev in range(8)])]
    psum x2 -> x0, waiting for transfers between devices: 542 us -> none  [shards(): factor = lax.psum(local_factor, 'tm')]
    add x0 -> x6, other arithmetic: none -> 66.8 us  [shards(): factor + lax.ppermute(factor, 'tm', [(dev, dev ^ hop) for dev in range(8)])]
  transfers between devices with their start and end apart: 6 -> 10, of which waited for: 6 -> 10; matrix products, arithmetic and copies ran while one was open for 0% -> 0% of each run, Pallas kernels for 0% -> 0%
where the time goes in v1:
time: 2110 us; the launch traced here: 2100 us
  waiting for transfers between devices  1590 us (75%)
  other arithmetic  308 us (15%)
  matrix products  113 us (5%)
  blocking collectives  38.6 us (2%)
  local copies, waits for them, and re-layouts  28.4 us (1%)
    ppermute x6, waiting for transfers between devices, shards(): lax.ppermute(factor, 'tm', [(dev, dev ^ hop) for dev in range(8)])  1440 us
    another operation x29, other arithmetic, shards(): lower = jnp.linalg.cholesky(gram)  158 us
    another operation x5, other arithmetic, shards(): lax.linalg.triangular_solve(lower, factor, left_side=False, lower=True, t...  79.2 us
    psum x2, waiting for transfers between devices, shards(): gram = lax.psum(local_gram, 'chan')  73.7 us
    add x6, other arithmetic, shards(): factor + lax.ppermute(factor, 'tm', [(dev, dev ^ hop) for dev in range(8)])  66.8 us
  transfers between devices with their start and end apart: 10, of which 10 were waited for; matrix products, arithmetic and copies ran while one was open for 0% of the time, Pallas kernels for 0%

profile of v1, /device:TPU:0, one launch (start us, length us, event | category | flops | bytes accessed | tf_op | source)
XLA Modules:
  0.0 2103.8 jit_solution(16649953715498821098)
XLA Ops:
  14.0 38.9 %all-reduce.7.cloned.1.call-done = f32[512,512]{1,0:T(8,128)} async-done(((f32[512,512]{1,0:T(8,128)}), f32[512,512]{1,0:T(8,128)}) %all-reduce.7.cloned.1.call-update) | async-done | bytes 1048592 | tf_op jit(solution)/shard_map/psum | solution.py:11
  62.6 180.6 %collective-permute-done = f32[4096,512]{0,1:T(8,128)} collective-permute-done((f32[4096,512]{0,1:T(8,128)S(1)}, f32[4096,512]{0,1:T(8,128)}, u32[]{:S(2)}, u32[]{:S(2)}) %collective-permute-start) | collective-permute-done | bytes 8388640 | tf_op jit(solution)/shard_map/ppermute | solution.py:21
  243.3 11.1 add.69
  255.6 180.1 %collective-permute-done.1 = f32[4096,512]{0,1:T(8,128)} collective-permute-done((f32[4096,512]{0,1:T(8,128)}, f32[4096,512]{0,1:T(8,128)}, u32[]{:S(2)}, u32[]{:S(2)}) %collective-permute-start.1) | collective-permute-done | bytes 8388640 | tf_op jit(solution)/shard_map/ppermute | solution.py:21
  435.8 11.1 add.70
  448.8 359.2 %collective-permute-done.2 = f32[4096,512]{0,1:T(8,128)} collective-permute-done((f32[4096,512]{0,1:T(8,128)}, f32[4096,512]{0,1:T(8,128)}, u32[]{:S(2)}, u32[]{:S(2)}) %collective-permute-start.2) | collective-permute-done | bytes 8388640 | tf_op jit(solution)/shard_map/ppermute | solution.py:21
  808.0 11.1 add.71
  819.2 17.2 fusion.85
  836.7 36.6 %all-reduce.9.cloned.1.call-done = f32[512,512]{0,1:T(8,128)} async-done(((f32[512,512]{0,1:T(8,128)}), f32[512,512]{0,1:T(8,128)}) %all-reduce.9.cloned.1.call-update) | async-done | bytes 1048592 | tf_op jit(solution)/shard_map/psum | solution.py:25
  876.3 11.7 cholesky.286
  898.7 11.7 cholesky.305
  910.4 10.2 custom-call.28
  921.3 11.7 cholesky.326
  944.1 11.7 cholesky.343
  967.6 39.3 %custom-call.30 = f32[4,128,128]{1,2,0:T(8,128)S(1)} custom-call(f32[4,128,128]{2,1,0:T(8,128)S(1)} %get-tuple-element.18), custom_call_target="InvertDiagBlocksLowerTriangular" | custom-call | tf_op jit(solution)/shard_map/triangular_solve/custom-call.3 | solution.py:27
  1031.0 25.7 %all-reduce.14 = bf16[512,512]{0,1:T(8,128)(2,1)} all-reduce(f32[512,512]{0,1:T(8,128)S(1)} %convolution_bitcast_fusion.3), channel_id=1, replica_groups=mesh['tm'=8,'chan'=4] {'chan'}, use_global_device_ids=true, to_apply=%region_10.13 | all-reduce | flops 262144 | bytes 1572864 | tf_op jit(solution)/shard_map/psum | solution.py:31
  1079.0 179.5 %collective-permute-done.3 = f32[4096,512]{0,1:T(8,128)} collective-permute-done((f32[4096,512]{0,1:T(8,128)S(1)}, f32[4096,512]{0,1:T(8,128)}, u32[]{:S(2)}, u32[]{:S(2)}) %collective-permute-start.3) | collective-permute-done | bytes 8388640 | tf_op jit(solution)/shard_map/ppermute | solution.py:21
  1258.6 11.1 add.73
  1271.2 179.1 %collective-permute-done.4 = f32[4096,512]{0,1:T(8,128)} collective-permute-done((f32[4096,512]{0,1:T(8,128)}, f32[4096,512]{0,1:T(8,128)}, u32[]{:S(2)}, u32[]{:S(2)}) %collective-permute-start.4) | collective-permute-done | bytes 8388640 | tf_op jit(solution)/shard_map/ppermute | solution.py:21
  1450.3 11.1 add.74
  1463.6 358.2 %collective-permute-done.5 = f32[4096,512]{0,1:T(8,128)} collective-permute-done((f32[4096,512]{0,1:T(8,128)}, f32[4096,512]{0,1:T(8,128)}, u32[]{:S(2)}, u32[]{:S(2)}) %collective-permute-start.5) | collective-permute-done | bytes 8388640 | tf_op jit(solution)/shard_map/ppermute | solution.py:21
  1821.8 11.1 add.75
  1832.9 17.2 fusion.86
  1850.4 37.1 %all-reduce.11.cloned.1.call-done = f32[512,512]{0,1:T(8,128)} async-done(((f32[512,512]{0,1:T(8,128)}), f32[512,512]{0,1:T(8,128)}) %all-reduce.11.cloned.1.call-update) | async-done | bytes 1048592 | tf_op jit(solution)/shard_map/psum | solution.py:25
  1890.6 11.7 cholesky.358
  1902.4 9.8 custom-call.31
  1912.9 11.7 cholesky.377
  1925.9 10.2 custom-call.32
  1936.8 11.7 cholesky.398
  1959.6 11.7 cholesky.415
  1982.4 39.3 %custom-call.34 = f32[4,128,128]{1,2,0:T(8,128)S(1)} custom-call(f32[4,128,128]{2,1,0:T(8,128)S(1)} %get-tuple-element.19), custom_call_target="InvertDiagBlocksLowerTriangular" | custom-call | tf_op jit(solution)/shard_map/triangular_solve/custom-call.3 | solution.py:27
  2046.9 36.6 %all-reduce.13.cloned.1.call-done = f32[512,512]{0,1:T(8,128)} async-done(((f32[512,512]{0,1:T(8,128)}), f32[512,512]{0,1:T(8,128)}) %all-reduce.13.cloned.1.call-update) | async-done | bytes 1048592 | tf_op jit(solution)/shard_map/psum | solution.py:31
  (148 shorter events, 184.1 us)
Async XLA Ops:
  7.2 45.8 %all-reduce.7.cloned.1.call-start = ((), (), s32[]{:S(2)}) async-start(), calls=%async_computation | async-start | bytes 2097152 | tf_op jit(solution)/shard_map/psum | solution.py:11
  14.0 859.3 %all-reduce.9.cloned.1.call-start = ((), (), s32[]{:S(2)}) async-start(), calls=%async_computation.1 | async-start | bytes 2097152 | tf_op jit(solution)/shard_map/psum | solution.py:25
  58.0 3.2 copy-start.1
  61.2 182.1 %collective-permute-start = (f32[4096,512]{0,1:T(8,128)S(1)}, f32[4096,512]{0,1:T(8,128)}, u32[]{:S(2)}, u32[]{:S(2)}) collective-permute-start(f32[4096,512]{0,1:T(8,128)S(1)} %convolution_bitcast_fusion.1), channel_id=1, source_target_pairs={{0,4},{4,0},{8,12},{12,8},{16,20},{20,16},{24,28},{28,24},{1,5},{5... | collective-permute-start | bytes 25165832 | tf_op jit(solution)/shard_map/ppermute | solution.py:21
  254.4 181.4 %collective-permute-start.1 = (f32[4096,512]{0,1:T(8,128)}, f32[4096,512]{0,1:T(8,128)}, u32[]{:S(2)}, u32[]{:S(2)}) collective-permute-start(f32[4096,512]{0,1:T(8,128)} %add.69), channel_id=1, source_target_pairs={{0,8},{4,12},{8,0},{12,4},{16,24},{20,28},{24,16},{28,20},{1,9},{5... | collective-permute-start | bytes 25165832 | tf_op jit(solution)/shard_map/ppermute | solution.py:21
  446.9 361.1 %collective-permute-start.2 = (f32[4096,512]{0,1:T(8,128)}, f32[4096,512]{0,1:T(8,128)}, u32[]{:S(2)}, u32[]{:S(2)}) collective-permute-start(f32[4096,512]{0,1:T(8,128)} %add.70), channel_id=1, source_target_pairs={{0,16},{4,20},{8,24},{12,28},{16,0},{20,4},{24,8},{28,12},{1,17},{... | collective-permute-start | bytes 25165832 | tf_op jit(solution)/shard_map/ppermute | solution.py:21
  836.4 1051.1 %all-reduce.11.cloned.1.call-start = ((), (), s32[]{:S(2)}) async-start(), calls=%async_computation.2 | async-start | bytes 2097152 | tf_op jit(solution)/shard_map/psum | solution.py:25
  1010.4 8.4 slice-start
  1012.4 6.4 slice-start.1
  1016.3 11.4 copy-start.3
  1020.9 6.7 copy-start.7
  1025.5 3.1 copy-start.4
  1027.6 1.0 copy-start.11
  1056.6 12.7 copy-start.8
  1074.0 3.2 copy-start
  1077.2 181.3 %collective-permute-start.3 = (f32[4096,512]{0,1:T(8,128)S(1)}, f32[4096,512]{0,1:T(8,128)}, u32[]{:S(2)}, u32[]{:S(2)}) collective-permute-start(f32[4096,512]{0,1:T(8,128)S(1)} %convolution_bitcast_fusion), channel_id=1, source_target_pairs={{0,4},{4,0},{8,12},{12,8},{16,20},{20,16},{24,28},{28,24},{1,5},{5... | collective-permute-start | bytes 25165832 | tf_op jit(solution)/shard_map/ppermute | solution.py:21
  1269.7 180.6 %collective-permute-start.4 = (f32[4096,512]{0,1:T(8,128)}, f32[4096,512]{0,1:T(8,128)}, u32[]{:S(2)}, u32[]{:S(2)}) collective-permute-start(f32[4096,512]{0,1:T(8,128)} %add.73), channel_id=1, source_target_pairs={{0,8},{4,12},{8,0},{12,4},{16,24},{20,28},{24,16},{28,20},{1,9},{5... | collective-permute-start | bytes 25165832 | tf_op jit(solution)/shard_map/ppermute | solution.py:21
  1461.4 360.4 %collective-permute-start.5 = (f32[4096,512]{0,1:T(8,128)}, f32[4096,512]{0,1:T(8,128)}, u32[]{:S(2)}, u32[]{:S(2)}) collective-permute-start(f32[4096,512]{0,1:T(8,128)} %add.74), channel_id=1, source_target_pairs={{0,16},{4,20},{8,24},{12,28},{16,0},{20,4},{24,8},{28,12},{1,17},{... | collective-permute-start | bytes 25165832 | tf_op jit(solution)/shard_map/ppermute | solution.py:21
  1850.2 233.3 %all-reduce.13.cloned.1.call-start = ((), (), s32[]{:S(2)}) async-start(), calls=%async_computation.3 | async-start | bytes 2097152 | tf_op jit(solution)/shard_map/psum | solution.py:31
  2025.3 8.4 slice-start.2
  2027.3 6.4 slice-start.3
  2031.1 11.4 copy-start.2
  2035.8 6.7 copy-start.6
  2040.4 3.1 copy-start.5
  2042.5 1.0 copy-start.10
  2083.4 12.3 copy-start.9
Sparse Core Ops, SparseCore 0:
  14.1 38.8 all-reduce.6
  836.5 36.6 all-reduce.8
  1850.3 37.1 all-reduce.10
  2047.0 36.4 all-reduce.12
